TPU v7x, 32 devices: a whole 2x2x4 slice. The times are simulated.
32 devices in a mesh: dp: 8 (over y, x, core), mp: 4 (over z).
Axes of the slice: x: 2, y: 2, z: 4, core: 2. Of those that a mesh axis runs over, the one named last changes fastest.
Arguments:
- frames: bfloat16 [8192, 1024], P(('dp', 'mp')), may hold values from -6 to 6
- lengths: int32 [8, 6], P('dp'), may hold values from 1 to 682, 896 in all within a row
- w_qkv: bfloat16 [3, 1024, 1024], P(None, None, 'mp'), may hold values from -0.1875 to 0.1875
- w_attn_out: bfloat16 [1024, 1024], P('mp'), may hold values from -0.5 to 0.5
- w_in: bfloat16 [1024, 4096], P(None, 'mp'), may hold values from -0.1875 to 0.1875
- w_out: bfloat16 [4096, 1024], P('mp'), may hold values from -0.09375 to 0.09375
- gain_attn: float32 [1024], replicated, may hold values from 0.5 to 1.5
- gain_mlp: float32 [1024], replicated, may hold values from 0.5 to 1.5
- cotangent: bfloat16 [8192, 1024], P(('dp', 'mp')), may hold values from -6 to 6
Outputs:
- output: bfloat16 [8192, 1024], P(('dp', 'mp'))
- grad_frames: float32 [8192, 1024], P(('dp', 'mp'))
- grad_w_qkv: float32 [3, 1024, 1024], P(None, None, 'mp')
- grad_w_attn_out: float32 [1024, 1024], P('mp')
- grad_w_in: float32 [1024, 4096], P(None, 'mp')
- grad_w_out: float32 [4096, 1024], P('mp')
- grad_gain_attn: float32 [1024], replicated
- grad_gain_mlp: float32 [1024], replicated
Inputs may be any that keep to these rules, and one draw needn't show every extreme that they name: `lengths`: each row holds the frame counts of the 6 items of one batch; they sum to 896 and the largest is exactly 682; the remaining frames of the batch are padding.
All inputs are finite; a program needn't handle non-finite values.
Results may differ from a plain program's by a relative error of at most 0.012.
Values may be sent and summed in bfloat16 or wider, within the bound.
A program may use at most 128 MiB of HBM per device.

v0:
```python
import jax
import jax.numpy as jnp
from jax import lax
from jax.sharding import PartitionSpec as P

HEAD = 64
BLOCK = 512
EPSILON = 1e-06
NEGATIVE = -1e30


def rms_scale(values, scaling_gain):
    return (
        values
        * lax.rsqrt(jnp.mean(values * values, axis=-1, keepdims=True) + EPSILON)
        * scaling_gain
    )


def gelu_tanh(values):
    return jax.nn.gelu(values, approximate=True)


def item_ids(length_row, frame_count):
    item_ends = jnp.cumsum(length_row)
    positions = jnp.arange(frame_count, dtype=jnp.int32)
    before = jnp.sum((positions[:, None] >= item_ends[None, :]).astype(jnp.int32), axis=1)
    return jnp.where(positions < item_ends[-1], before, before + positions + 1)


def block_scores(queries, positions, idents, keys_all, idents_all, scaling):
    scores = (
        jnp.einsum("bhd,khd->hbk", queries, keys_all, preferred_element_type=jnp.float32) * scaling
    )
    frame_count = keys_all.shape[0]
    visible = (idents[:, None] == idents_all[None, :]) & (
        jnp.arange(frame_count, dtype=jnp.int32)[None, :] <= positions[:, None]
    )
    return (scores, visible[None])


def per_device(frames, lengths, w_qkv, w_attn_out, w_in, w_out, gain_attn, gain_mlp, cotangent):
    frame_count = frames.shape[0] * lax.axis_size("mp")
    heads_here = w_attn_out.shape[0] // HEAD
    scaling = HEAD ** (-0.5)
    idents = item_ids(lengths[0], frame_count)
    positions = jnp.arange(frame_count, dtype=jnp.int32)
    frames_wide = frames.astype(jnp.float32)
    normed = rms_scale(frames_wide, gain_attn).astype(jnp.bfloat16)
    normed_all = lax.all_gather(normed, "mp", axis=0, tiled=True)
    projected = jnp.einsum(
        "td,cde->cte", normed_all, w_qkv, preferred_element_type=jnp.float32
    ).astype(jnp.bfloat16)
    head_split = projected.reshape(3, frame_count, heads_here, HEAD)
    queries, keys_all, values_all = (head_split[0], head_split[1], head_split[2])
    blocks = frame_count // BLOCK
    outputs = []
    log_totals = []
    for number in range(blocks):
        window = slice(number * BLOCK, (number + 1) * BLOCK)
        scores, visible = block_scores(
            queries[window], positions[window], idents[window], keys_all, idents, scaling
        )
        masked = jnp.where(visible, scores, NEGATIVE)
        row_peak = jnp.max(masked, axis=-1, keepdims=True)
        weights = jnp.where(visible, jnp.exp(masked - row_peak), 0.0)
        row_total = jnp.sum(weights, axis=-1, keepdims=True)
        probabilities = weights / row_total
        outputs.append(
            jnp.einsum(
                "hbk,khd->bhd",
                probabilities.astype(jnp.bfloat16),
                values_all,
                preferred_element_type=jnp.float32,
            )
        )
        log_totals.append(row_peak + jnp.log(row_total))
    attended = (
        jnp.concatenate(outputs, axis=0)
        .reshape(frame_count, heads_here * HEAD)
        .astype(jnp.bfloat16)
    )
    attn_part = jnp.dot(attended, w_attn_out, preferred_element_type=jnp.float32)
    attn_own = lax.psum_scatter(attn_part, "mp", scatter_dimension=0, tiled=True)
    resid = frames_wide + attn_own
    normed_mlp = rms_scale(resid, gain_mlp).astype(jnp.bfloat16)
    normed_mlp_all = lax.all_gather(normed_mlp, "mp", axis=0, tiled=True)
    hidden = jnp.dot(normed_mlp_all, w_in, preferred_element_type=jnp.float32)
    active = gelu_tanh(hidden).astype(jnp.bfloat16)
    mlp_own = lax.psum_scatter(
        jnp.dot(active, w_out, preferred_element_type=jnp.float32).astype(jnp.bfloat16),
        "mp",
        scatter_dimension=0,
        tiled=True,
    ).astype(jnp.float32)
    output = (resid + mlp_own).astype(jnp.bfloat16)
    grad_top = cotangent.astype(jnp.float32)
    grad_all = lax.all_gather(cotangent, "mp", axis=0, tiled=True)
    grad_w_out = jnp.einsum("tf,td->fd", active, grad_all, preferred_element_type=jnp.float32)
    grad_active = jnp.einsum("td,fd->tf", grad_all, w_out, preferred_element_type=jnp.float32)
    grad_hidden = jax.vjp(gelu_tanh, hidden)[1](grad_active)[0].astype(jnp.bfloat16)
    grad_w_in = jnp.einsum(
        "td,tf->df", normed_mlp_all, grad_hidden, preferred_element_type=jnp.float32
    )
    grad_normed_mlp = lax.psum_scatter(
        jnp.einsum("tf,df->td", grad_hidden, w_in, preferred_element_type=jnp.float32),
        "mp",
        scatter_dimension=0,
        tiled=True,
    )
    resid_back, gain_mlp_part = jax.vjp(rms_scale, resid, gain_mlp)[1](grad_normed_mlp)
    grad_resid = grad_top + resid_back
    grad_resid_all = lax.all_gather(grad_resid.astype(jnp.bfloat16), "mp", axis=0, tiled=True)
    grad_w_attn_out = jnp.einsum(
        "te,td->ed", attended, grad_resid_all, preferred_element_type=jnp.float32
    )
    grad_attended = (
        jnp.einsum("td,ed->te", grad_resid_all, w_attn_out, preferred_element_type=jnp.float32)
        .astype(jnp.bfloat16)
        .reshape(frame_count, heads_here, HEAD)
    )
    grad_keys = jnp.zeros((frame_count, heads_here, HEAD), jnp.float32)
    grad_values = jnp.zeros((frame_count, heads_here, HEAD), jnp.float32)
    grad_queries = []
    for number in range(blocks):
        window = slice(number * BLOCK, (number + 1) * BLOCK)
        scores, visible = block_scores(
            queries[window], positions[window], idents[window], keys_all, idents, scaling
        )
        probabilities = jnp.where(
            visible, jnp.exp(jnp.where(visible, scores, NEGATIVE) - log_totals[number]), 0.0
        )
        grad_rows = grad_attended[window]
        grad_probs = jnp.einsum(
            "bhd,khd->hbk", grad_rows, values_all, preferred_element_type=jnp.float32
        )
        grad_values = grad_values + jnp.einsum(
            "hbk,bhd->khd",
            probabilities.astype(jnp.bfloat16),
            grad_rows,
            preferred_element_type=jnp.float32,
        )
        inner_sum = jnp.sum(probabilities * grad_probs, axis=-1, keepdims=True)
        grad_scores = (probabilities * (grad_probs - inner_sum)).astype(jnp.bfloat16)
        grad_queries.append(
            jnp.einsum("hbk,khd->bhd", grad_scores, keys_all, preferred_element_type=jnp.float32)
            * scaling
        )
        grad_keys = (
            grad_keys
            + jnp.einsum(
                "hbk,bhd->khd", grad_scores, queries[window], preferred_element_type=jnp.float32
            )
            * scaling
        )
    grad_projected = jnp.stack(
        [
            jnp.concatenate(grad_queries, axis=0).reshape(frame_count, heads_here * HEAD),
            grad_keys.reshape(frame_count, heads_here * HEAD),
            grad_values.reshape(frame_count, heads_here * HEAD),
        ]
    ).astype(jnp.bfloat16)
    grad_w_qkv = jnp.einsum(
        "td,cte->cde", normed_all, grad_projected, preferred_element_type=jnp.float32
    )
    grad_normed = lax.psum_scatter(
        jnp.einsum("cte,cde->td", grad_projected, w_qkv, preferred_element_type=jnp.float32),
        "mp",
        scatter_dimension=0,
        tiled=True,
    )
    frames_back, gain_attn_part = jax.vjp(rms_scale, frames_wide, gain_attn)[1](grad_normed)
    grad_frames = grad_resid + frames_back
    grad_gain_attn, grad_gain_mlp = lax.psum((gain_attn_part, gain_mlp_part), ("dp", "mp"))
    grad_w_qkv, grad_w_attn_out, grad_w_in, grad_w_out = lax.psum(
        (grad_w_qkv, grad_w_attn_out, grad_w_in, grad_w_out), "dp"
    )
    return (
        output,
        grad_frames,
        grad_w_qkv,
        grad_w_attn_out,
        grad_w_in,
        grad_w_out,
        grad_gain_attn,
        grad_gain_mlp,
    )


def solution(mesh):
    in_specs = (
        P(("dp", "mp"), None),
        P("dp", None),
        P(None, None, "mp"),
        P("mp", None),
        P(None, "mp"),
        P("mp", None),
        P(),
        P(),
        P(("dp", "mp"), None),
    )
    out_specs = (
        P(("dp", "mp"), None),
        P(("dp", "mp"), None),
        P(None, None, "mp"),
        P("mp", None),
        P(None, "mp"),
        P("mp", None),
        P(),
        P(),
    )
    return jax.shard_map(
        per_device, mesh=mesh, in_specs=in_specs, out_specs=out_specs, check_vma=False
    )
```

profile of v0, /device:TPU:0, one launch (start us, length us, event | category | flops | bytes accessed | tf_op | source)
XLA Modules:
  0.0 765.5 jit_solution(12484631126287785952)
XLA Ops:
  14.7 44.8 %all-gather.5.cloned.1.call-done = bf16[1024,1024]{1,0:T(8,128)(2,1)} async-done(((bf16[256,1024]{1,0:T(8,128)(2,1)}), bf16[1024,1024]{1,0:T(8,128)(2,1)}) %all-gather.5.cloned.1.call-update) | async-done | bytes 2097168 | tf_op jit(solution)/shard_map/all_gather | solution.py:50
  59.5 3.9 fusion.29
  84.2 74.4 %reduce-scatter.5.cloned.1.call-done = f32[256,1024]{1,0:T(8,128)} async-done(((f32[1024,1024]{1,0:T(8,128)}), f32[256,1024]{1,0:T(8,128)}) %reduce-scatter.5.cloned.1.call-update) | async-done | bytes 1048592 | tf_op jit(solution)/shard_map/reduce_scatter | solution.py:84
  161.2 45.5 %all-gather.9.cloned.1.call-done = bf16[1024,1024]{1,0:T(8,128)(2,1)} async-done(((bf16[256,1024]{1,0:T(8,128)(2,1)}), bf16[1024,1024]{1,0:T(8,128)(2,1)}) %all-gather.9.cloned.1.call-update) | async-done | bytes 2097168 | tf_op jit(solution)/shard_map/all_gather | solution.py:98
  206.8 6.6 fusion.79
  213.4 40.2 %all-gather.7.cloned.1.call-done = bf16[1024,1024]{1,0:T(8,128)(2,1)} async-done(((bf16[256,1024]{1,0:T(8,128)(2,1)}), bf16[1024,1024]{1,0:T(8,128)(2,1)}) %all-gather.7.cloned.1.call-update) | async-done | bytes 2097168 | tf_op jit(solution)/shard_map/all_gather | solution.py:87
  253.5 8.2 %fusion.10 = (bf16[1024,1024]{1,0:T(8,128)(2,1)S(1)}, f32[1024,1024]{1,0:T(8,128)}) fusion(f32[1024,1024]{1,0:T(8,128)} %fusion.79, bf16[1024,1024]{1,0:T(8,128)(2,1)} %all-gather.7.cloned.1.call-done, bf16[1024,1024]{1,0:T(8,128)(2,1)S(1)} %copy-done), kind=kOutput, calls=%fused_computation.24 | convolution fusion | flops 2168455168 | bytes 14680064 | tf_op jit(solution)/shard_map/dot_general | solution.py:88
  263.1 4.4 fusion.80
  267.6 75.6 %reduce-scatter.9.cloned.1.call-done = f32[256,1024]{1,0:T(8,128)} async-done(((f32[1024,1024]{1,0:T(8,128)}), f32[256,1024]{1,0:T(8,128)}) %reduce-scatter.9.cloned.1.call-update) | async-done | bytes 1048592 | tf_op jit(solution)/shard_map/reduce_scatter | solution.py:105
  347.3 6.7 fusion.83
  354.0 4.8 fusion.73
  358.8 34.8 %all-gather.11.cloned.1.call-done = bf16[1024,1024]{1,0:T(8,128)(2,1)} async-done(((bf16[256,1024]{1,0:T(8,128)(2,1)}), bf16[1024,1024]{1,0:T(8,128)(2,1)}) %all-gather.11.cloned.1.call-update) | async-done | bytes 2097168 | tf_op jit(solution)/shard_map/all_gather | solution.py:113
  396.2 5.2 fusion.11
  401.5 5.7 multiply_reduce_fusion
  407.2 5.8 multiply_reduce_fusion.1
  413.0 10.5 %multiply_convert_fusion = (bf16[4,512,1024]{2,1,0:T(8,128)(2,1)}, bf16[4,512,1024]{2,1,0:T(8,128)(2,1)S(1)}) fusion(f32[4,512,1024]{2,1,0:T(8,128)} %get-tuple-element.57, f32[4,512]{1,0:T(4,128)S(1)} %get-tuple-element.56, f32[4,512]{1,0:T(4,128)S(1)} %log_add_fusion, f32[4,512,1024]{2,1,0:T(8,128)S(1)} %bitcast.83, pred[512,1024]{1,0:T(8,128)(4,1)S(1)} %copy-done.12, ...), kind=kLoop, calls=%fused_computation | loop fusion | flops 29360128 | bytes 43024384 | tf_op jit(solution)/shard_map/convert_element_type | solution.py:144
  431.8 4.4 fusion.48
  443.6 5.3 fusion.23
  449.9 5.2 convolution_bitcast_fusion
  456.8 6.3 convolution_convert_fusion
  463.1 158.1 %all-reduce.4.cloned.1.call-done = (f32[3,1024,256]{1,2,0:T(8,128)}, f32[256,1024]{1,0:T(8,128)}, f32[1024,1024]{1,0:T(8,128)}, f32[1024,1024]{1,0:T(8,128)}) async-done(((f32[3,1024,256]{1,2,0:T(8,128)}, f32[256,1024]{1,0:T(8,128)}, f32[1024,1024]{1,0:T(8,128)}, f32[1024,1024]{1,0:T(8,128)}), (f32[3,1024,256]{1,2,0:T(8,128)}, f32[256,1024]{1,0:T(8,128)}, f32[1024,1024]{1,0:T(8,128)}, ...) | async-done | bytes 12582928 | tf_op jit(solution)/shard_map/psum | solution.py:175
  621.2 3.5 copy.28
  624.7 76.3 %reduce-scatter.11.cloned.1.call-done = f32[256,1024]{1,0:T(8,128)} async-done(((f32[1024,1024]{1,0:T(8,128)}), f32[256,1024]{1,0:T(8,128)}) %reduce-scatter.11.cloned.1.call-update) | async-done | bytes 1048592 | tf_op jit(solution)/shard_map/reduce_scatter | solution.py:166
  702.6 43.7 %all-reduce = (f32[1024]{0:T(1024)}, f32[1024]{0:T(1024)}) all-reduce(f32[1024]{0:T(1024)S(1)} %get-tuple-element.26, f32[1024]{0:T(1024)S(1)} %get-tuple-element.24), channel_id=1, replica_groups=mesh['dp'=8,'mp'=4] {'dp','mp'}, use_global_device_ids=true, to_apply=%region_21.22 | all-reduce | flops 2048 | bytes 16384 | tf_op jit(solution)/shard_map/psum | solution.py:174
  (147 shorter events, 70.8 us)
Async XLA Ops:
  7.2 246.4 %copy-start = (bf16[1024,1024]{1,0:T(8,128)(2,1)S(1)}, bf16[1024,1024]{1,0:T(8,128)(2,1)}, u32[]{:S(2)}) copy-start(bf16[1024,1024]{1,0:T(8,128)(2,1)} %param.13) | copy-start | bytes 6291460
  7.2 52.3 %all-gather.5.cloned.1.call-start = ((), (), s32[]{:S(2)}) async-start(), calls=%async_computation.4 | async-start | bytes 2621440 | tf_op jit(solution)/shard_map/all_gather | solution.py:50
  10.7 148.0 %reduce-scatter.5.cloned.1.call-start = ((), (), s32[]{:S(2)}) async-start(), calls=%async_computation.5 | async-start | bytes 5242880 | tf_op jit(solution)/shard_map/reduce_scatter | solution.py:84
  14.7 61.7 %copy-start.9 = (pred[512,1024]{1,0:T(8,128)(4,1)}, pred[512,1024]{1,0:T(8,128)(4,1)S(1)}, u32[]{:S(2)}) copy-start(pred[512,1024]{1,0:T(8,128)(4,1)S(1)} %get-tuple-element.44) | copy-start | bytes 1572868
  63.4 8.4 %copy-start.19 = (bf16[1,512,256]{1,2,0:T(8,128)(2,1)}, bf16[1,512,256]{1,2,0:T(8,128)(2,1)S(1)}, u32[]{:S(2)}) copy-start(bf16[1,512,256]{1,2,0:T(8,128)(2,1)S(1)} %get-tuple-element.36) | copy-start | bytes 786436
  63.5 8.3 %copy-start.5 = (bf16[1,1024,256]{1,2,0:T(8,128)(2,1)}, bf16[1,1024,256]{1,2,0:T(8,128)(2,1)S(1)}, u32[]{:S(2)}) copy-start(bf16[1,1024,256]{1,2,0:T(8,128)(2,1)S(1)} %get-tuple-element.38) | copy-start | bytes 1572868
  63.5 12.9 %copy-start.27 = (bf16[1,1024,256]{1,2,0:T(8,128)(2,1)}, bf16[1,1024,256]{1,2,0:T(8,128)(2,1)S(1)}, u32[]{:S(2)}) copy-start(bf16[1,1024,256]{1,2,0:T(8,128)(2,1)S(1)} %get-tuple-element.39) | copy-start | bytes 1572868
  83.0 77.2 %copy-start.29 = (f32[1024]{0:T(1024)S(1)}, f32[1024]{0:T(1024)}, u32[]{:S(2)}) copy-start(f32[1024]{0:T(1024)} %param.16) | copy-start | bytes 12292
  83.0 123.8 %all-gather.9.cloned.1.call-start = ((), (), s32[]{:S(2)}) async-start(), calls=%async_computation.8 | async-start | bytes 2621440 | tf_op jit(solution)/shard_map/all_gather | solution.py:98
  83.7 169.8 %all-gather.7.cloned.1.call-start = ((), (), s32[]{:S(2)}) async-start(), calls=%async_computation.6 | async-start | bytes 2621440 | tf_op jit(solution)/shard_map/all_gather | solution.py:87
  161.2 182.0 %reduce-scatter.9.cloned.1.call-start = ((), (), s32[]{:S(2)}) async-start(), calls=%async_computation.9 | async-start | bytes 5242880 | tf_op jit(solution)/shard_map/reduce_scatter | solution.py:105
  267.5 77.1 %copy-start.15 = (bf16[256,1024]{1,0:T(8,128)(2,1)S(1)}, bf16[256,1024]{1,0:T(8,128)(2,1)}, u32[]{:S(2)}) copy-start(bf16[256,1024]{1,0:T(8,128)(2,1)} %param.17) | copy-start | bytes 1572868
  267.6 126.1 %all-gather.11.cloned.1.call-start = ((), (), s32[]{:S(2)}) async-start(), calls=%async_computation.10 | async-start | bytes 2621440 | tf_op jit(solution)/shard_map/all_gather | solution.py:113
  347.0 274.1 %all-reduce.4.cloned.1.call-start = ((), (), s32[]{:S(2)}) async-start(), calls=%async_computation.12 | async-start | bytes 25165824 | tf_op jit(solution)/shard_map/psum | solution.py:175
  354.0 39.6 %copy-start.23 = (bf16[256,1024]{1,0:T(8,128)(2,1)S(1)}, bf16[256,1024]{1,0:T(8,128)(2,1)}, u32[]{:S(2)}) copy-start(bf16[256,1024]{1,0:T(8,128)(2,1)} %param.12) | copy-start | bytes 1572868
  358.8 37.3 %copy-start.12 = (pred[512,1024]{1,0:T(8,128)(4,1)S(1)}, pred[512,1024]{1,0:T(8,128)(4,1)}, u32[]{:S(2)}) copy-start(pred[512,1024]{1,0:T(8,128)(4,1)} %get-tuple-element.45) | copy-start | bytes 1572868
  396.2 11.0 %slice-start = ((s8[8388608]{0:T(1024)(128)(4,1)}), s8[4194304]{0:T(1024)(128)(4,1)S(1)}, s32[]{:S(2)}) async-start(s8[8388608]{0:T(1024)(128)(4,1)} %bitcast.80), calls=%async_computation.13 | async-start | bytes 8388608
  413.0 10.5 %copy-start.6 = (bf16[1,1024,256]{1,2,0:T(8,128)(2,1)S(1)}, bf16[1,1024,256]{1,2,0:T(8,128)(2,1)}, u32[]{:S(2)}) copy-start(bf16[1,1024,256]{1,2,0:T(8,128)(2,1)} %copy-done.5) | copy-start | bytes 1572868
  448.9 252.1 %reduce-scatter.11.cloned.1.call-start = ((), (), s32[]{:S(2)}) async-start(), calls=%async_computation.11 | async-start | bytes 5242880 | tf_op jit(solution)/shard_map/reduce_scatter | solution.py:166
  455.2 293.6 %reduce-scatter.7.cloned.1.call-start = ((), (), s32[]{:S(2)}) async-start(), calls=%async_computation.7 | async-start | bytes 2621440 | tf_op jit(solution)/shard_map/reduce_scatter | solution.py:90
  463.0 238.0 %copy-start.7 = (bf16[256,1024]{1,0:T(8,128)(2,1)S(1)}, bf16[256,1024]{1,0:T(8,128)(2,1)}, u32[]{:S(2)}) copy-start(bf16[256,1024]{1,0:T(8,128)(2,1)} %param.9) | copy-start | bytes 1572868
  463.0 238.0 %copy-start.30 = (f32[1024]{0:T(1024)S(1)}, f32[1024]{0:T(1024)}, u32[]{:S(2)}) copy-start(f32[1024]{0:T(1024)} %param.15) | copy-start | bytes 12292
  463.0 285.7 %copy-start.8 = (f32[256,1024]{1,0:T(8,128)S(1)}, f32[256,1024]{1,0:T(8,128)}, u32[]{:S(2)}) copy-start(f32[256,1024]{1,0:T(8,128)} %reduce-scatter.9.cloned.1.call-done) | copy-start | bytes 3145732
  463.1 285.7 %copy-start.16 = (bf16[256,1024]{1,0:T(8,128)(2,1)S(1)}, bf16[256,1024]{1,0:T(8,128)(2,1)}, u32[]{:S(2)}) copy-start(bf16[256,1024]{1,0:T(8,128)(2,1)} %param.17) | copy-start | bytes 1572868
  (24 other events, 103.1 us)
Sparse Core Ops, SparseCore 0:
  10.8 48.6 all-gather.4
  83.1 75.4 reduce-scatter.4
  160.3 46.4 all-gather.8
  208.8 44.6 all-gather.6
  267.7 75.4 reduce-scatter.8
  347.2 46.4 all-gather.10
  449.0 172.0 all-reduce.3
  624.1 76.8 reduce-scatter.10
  703.3 45.3 reduce-scatter.6
where the time goes:
time: 774 us; the launch traced here: 766 us
  waiting for transfers between devices  553 us (71%)
  matrix products  98.3 us (13%)
  blocking collectives  43.7 us (6%)
  other arithmetic  35.4 us (5%)
  local copies, waits for them, and re-layouts  19.6 us (3%)
  between operations  14.7 us (2%)
    psum x1, waiting for transfers between devices, per_device(): lax.psum((grad_w_qkv, grad_w_attn_out, grad_w_in, grad_w_out), 'dp')  158 us
    reduce_scatter x1, waiting for transfers between devices, per_device(): lax.psum_scatter(jnp.einsum('cte,cde->td', grad_projected, w_qkv, preferr...  76.3 us
    reduce_scatter x1, waiting for transfers between devices, per_device(): lax.psum_scatter(jnp.einsum('tf,df->td', grad_hidden, w_in, preferred_ele...  75.6 us
    reduce_scatter x1, waiting for transfers between devices, per_device(): lax.psum_scatter(attn_part, 'mp', scatter_dimension=0, tiled=True)  74.4 us
    all_gather x1, waiting for transfers between devices, per_device(): grad_all = lax.all_gather(cotangent, 'mp', axis=0, tiled=True)  45.5 us
    all_gather x1, waiting for transfers between devices, per_device(): normed_all = lax.all_gather(normed, 'mp', axis=0, tiled=True)  44.8 us
    psum x1, blocking collectives, per_device(): lax.psum((gain_attn_part, gain_mlp_part), ('dp', 'mp'))  43.7 us
    all_gather x1, waiting for transfers between devices, per_device(): normed_mlp_all = lax.all_gather(normed_mlp, 'mp', axis=0, tiled=True)  40.2 us
  transfers between devices with their start and end apart: 9, of which 9 were waited for; matrix products, arithmetic and copies ran while one was open for 5% of the time, Pallas kernels for 0%

commit v1 on v0

--- a/solution.py
+++ b/solution.py
@@ -95,7 +95,16 @@
     ).astype(jnp.float32)
     output = (resid + mlp_own).astype(jnp.bfloat16)
     grad_top = cotangent.astype(jnp.float32)
-    grad_all = lax.all_gather(cotangent, "mp", axis=0, tiled=True)
+    fan = lax.axis_size("mp")
+    tray = tuple(((nth, (nth + 1) % fan) for nth in range(fan)))
+    e_next = [None] * fan
+    e_next[fan - 1] = cotangent
+    for dev in range(fan - 2, -1, -1):
+        e_next[dev] = lax.ppermute(e_next[dev + 1], axis_name="mp", perm=tray)
+    d_next = jnp.concatenate(e_next, 0)
+    odd = lax.axis_index("mp")
+    right_arr = (odd + 1) * cotangent.shape[0]
+    grad_all = jnp.roll(d_next, right_arr, 0)
     grad_w_out = jnp.einsum("tf,td->fd", active, grad_all, preferred_element_type=jnp.float32)
     grad_active = jnp.einsum("td,fd->tf", grad_all, w_out, preferred_element_type=jnp.float32)
     grad_hidden = jax.vjp(gelu_tanh, hidden)[1](grad_active)[0].astype(jnp.bfloat16)

time: 774 us -> 772 us (level)
  waiting for transfers between devices: 553 us -> 516 us
  starting transfers between devices: 1.01 us -> 21.5 us
  local copies, waits for them, and re-layouts: 19.6 us -> 33.3 us
    ppermute x0 -> x3, waiting for transfers between devices: none -> 51 us  [per_device(): e_next[dev] = lax.ppermute(e_next[dev + 1], axis_name='mp', perm=tray)]
    all_gather x1 -> x0, waiting for transfers between devices: 45.5 us -> none  [per_device(): grad_all = lax.all_gather(cotangent, 'mp', axis=0, tiled=True)]
    all_gather x1, waiting for transfers between devices: 40.2 us -> 0.01 us  [per_device(): normed_mlp_all = lax.all_gather(normed_mlp, 'mp', axis=0, tiled=True)]
    ppermute x0 -> x3, starting transfers between devices: none -> 20.5 us  [per_device(): e_next[dev] = lax.ppermute(e_next[dev + 1], axis_name='mp', perm=tray)]
    unnamed x82 -> x97, local copies, waits for them, and re-layouts: 14.8 us -> 27.7 us
  transfers between devices with their start and end apart: 9 -> 11, of which waited for: 9 -> 10; matrix products, arithmetic and copies ran while one was open for 5% -> 6% of each run, Pallas kernels for 0% -> 0%
where the time goes in v1:
time: 772 us; the launch traced here: 762 us
  waiting for transfers between devices  516 us (67%)
  matrix products  97.3 us (13%)
  blocking collectives  43.7 us (6%)
  other arithmetic  35.4 us (5%)
  local copies, waits for them, and re-layouts  33.3 us (4%)
  starting transfers between devices  21.5 us (3%)
  between operations  15 us (2%)
    psum x1, waiting for transfers between devices, per_device(): lax.psum((grad_w_qkv, grad_w_attn_out, grad_w_in, grad_w_out), 'dp')  158 us
    reduce_scatter x1, waiting for transfers between devices, per_device(): lax.psum_scatter(jnp.einsum('cte,cde->td', grad_projected, w_qkv, preferr...  76.3 us
    reduce_scatter x1, waiting for transfers between devices, per_device(): lax.psum_scatter(jnp.einsum('tf,df->td', grad_hidden, w_in, preferred_ele...  75.3 us
    reduce_scatter x1, waiting for transfers between devices, per_device(): lax.psum_scatter(attn_part, 'mp', scatter_dimension=0, tiled=True)  75.1 us
    ppermute x3, waiting for transfers between devices, per_device(): e_next[dev] = lax.ppermute(e_next[dev + 1], axis_name='mp', perm=tray)  51 us
    all_gather x1, waiting for transfers between devices, per_device(): normed_all = lax.all_gather(normed, 'mp', axis=0, tiled=True)  44.8 us
    psum x1, blocking collectives, per_device(): lax.psum((gain_attn_part, gain_mlp_part), ('dp', 'mp'))  43.7 us
    all_gather x1, waiting for transfers between devices, per_device(): lax.all_gather(grad_resid.astype(jnp.bfloat16), 'mp', axis=0, tiled=True)  32.9 us
  transfers between devices with their start and end apart: 11, of which 10 were waited for; matrix products, arithmetic and copies ran while one was open for 6% of the time, Pallas kernels for 0%

profile of v1, /device:TPU:0, one launch (start us, length us, event | category | flops | bytes accessed | tf_op | source)
XLA Modules:
  0.0 762.3 jit_solution(13236756058929598485)
XLA Ops:
  14.7 44.8 %all-gather.4.cloned.1.call-done = bf16[1024,1024]{1,0:T(8,128)(2,1)} async-done(((bf16[256,1024]{1,0:T(8,128)(2,1)}), bf16[1024,1024]{1,0:T(8,128)(2,1)}) %all-gather.4.cloned.1.call-update) | async-done | bytes 2097168 | tf_op jit(solution)/shard_map/all_gather | solution.py:50
  83.5 75.1 %reduce-scatter.5.cloned.1.call-done = f32[256,1024]{1,0:T(8,128)} async-done(((f32[1024,1024]{1,0:T(8,128)}), f32[256,1024]{1,0:T(8,128)}) %reduce-scatter.5.cloned.1.call-update) | async-done | bytes 1048592 | tf_op jit(solution)/shard_map/reduce_scatter | solution.py:84
  162.8 18.2 %collective-permute-done = bf16[256,1024]{1,0:T(8,128)(2,1)S(1)} collective-permute-done((bf16[256,1024]{1,0:T(8,128)(2,1)}, bf16[256,1024]{1,0:T(8,128)(2,1)S(1)}, u32[]{:S(2)}, u32[]{:S(2)}) %collective-permute-start) | collective-permute-done | bytes 524320 | tf_op jit(solution)/shard_map/ppermute | solution.py:103
  181.8 6.2 collective-permute-start.1
  188.0 21.2 %collective-permute-done.1 = bf16[256,1024]{1,0:T(8,128)(2,1)} collective-permute-done((bf16[256,1024]{1,0:T(8,128)(2,1)S(1)}, bf16[256,1024]{1,0:T(8,128)(2,1)}, u32[]{:S(2)}, u32[]{:S(2)}) %collective-permute-start.1) | collective-permute-done | bytes 524320 | tf_op jit(solution)/shard_map/ppermute | solution.py:103
  209.2 12.8 %collective-permute-start.2 = (bf16[256,1024]{1,0:T(8,128)(2,1)}, bf16[256,1024]{1,0:T(8,128)(2,1)}, u32[]{:S(2)}, u32[]{:S(2)}) collective-permute-start(bf16[256,1024]{1,0:T(8,128)(2,1)} %collective-permute-done.1), channel_id=1, source_target_pairs={{0,1},{1,2},{2,3},{3,0},{4,5},{5,6},{6,7},{7,4},{8,9},{9,10},{10,1... | collective-permute-start | bytes 1572872 | tf_op jit(solution)/shard_map/ppermute | solution.py:103
  222.0 11.6 %collective-permute-done.2 = bf16[256,1024]{1,0:T(8,128)(2,1)} collective-permute-done((bf16[256,1024]{1,0:T(8,128)(2,1)}, bf16[256,1024]{1,0:T(8,128)(2,1)}, u32[]{:S(2)}, u32[]{:S(2)}) %collective-permute-start.2) | collective-permute-done | bytes 524320 | tf_op jit(solution)/shard_map/ppermute | solution.py:103
  250.5 8.0 %fusion.10 = bf16[1024,1024]{1,0:T(8,128)(2,1)S(1)} fusion(f32[1024,1024]{1,0:T(8,128)S(1)} %fusion.86, bf16[1024,1024]{1,0:T(8,128)(2,1)S(1)} %copy-done.34, bf16[2048,1024]{1,0:T(8,128)(2,1)} %constant_dynamic-update-slice_fusion, s32[]{:T(128)S(6)} %select_n.48), kind=kOutput, calls=%fused_computation.24 | convolution fusion | flops 2168455168 | bytes 10485764 | tf_op jit(solution)/shard_map/td,fd->tf/dot_general | solution.py:109
  259.8 4.4 fusion.87
  264.3 75.3 %reduce-scatter.9.cloned.1.call-done = f32[256,1024]{1,0:T(8,128)} async-done(((f32[1024,1024]{1,0:T(8,128)}), f32[256,1024]{1,0:T(8,128)}) %reduce-scatter.9.cloned.1.call-update) | async-done | bytes 1048592 | tf_op jit(solution)/shard_map/reduce_scatter | solution.py:114
  343.7 6.8 fusion.90
  350.5 6.6 fusion.26
  357.1 32.9 %all-gather.8.cloned.1.call-done = bf16[1024,1024]{1,0:T(8,128)(2,1)} async-done(((bf16[256,1024]{1,0:T(8,128)(2,1)}), bf16[1024,1024]{1,0:T(8,128)(2,1)}) %all-gather.8.cloned.1.call-update) | async-done | bytes 2097168 | tf_op jit(solution)/shard_map/all_gather | solution.py:122
  392.6 5.2 fusion.11
  397.8 5.8 multiply_reduce_fusion
  403.6 5.8 multiply_reduce_fusion.1
  409.4 10.5 %multiply_convert_fusion = (bf16[4,512,1024]{2,1,0:T(8,128)(2,1)}, bf16[4,512,1024]{2,1,0:T(8,128)(2,1)S(1)}) fusion(f32[4,512,1024]{2,1,0:T(8,128)} %get-tuple-element.55, f32[4,512]{1,0:T(4,128)S(1)} %get-tuple-element.54, f32[4,512]{1,0:T(4,128)S(1)} %log_add_fusion, f32[4,512,1024]{2,1,0:T(8,128)S(1)} %bitcast.81, pred[512,1024]{1,0:T(8,128)(4,1)S(1)} %copy-done.12, ...), kind=kLoop, calls=%fused_computation | loop fusion | flops 29360128 | bytes 43024384 | tf_op jit(solution)/shard_map/convert_element_type | solution.py:153
  428.2 4.4 fusion.54
  440.0 5.3 fusion.23
  446.3 5.2 convolution_bitcast_fusion
  453.2 6.2 convolution_convert_fusion
  459.5 158.1 %all-reduce.4.cloned.1.call-done = (f32[3,1024,256]{1,2,0:T(8,128)}, f32[256,1024]{1,0:T(8,128)}, f32[1024,1024]{1,0:T(8,128)}, f32[1024,1024]{1,0:T(8,128)}) async-done(((f32[3,1024,256]{1,2,0:T(8,128)}, f32[256,1024]{1,0:T(8,128)}, f32[1024,1024]{1,0:T(8,128)}, f32[1024,1024]{1,0:T(8,128)}), (f32[3,1024,256]{1,2,0:T(8,128)}, f32[256,1024]{1,0:T(8,128)}, f32[1024,1024]{1,0:T(8,128)}, ...) | async-done | bytes 12582928 | tf_op jit(solution)/shard_map/psum | solution.py:184
  621.1 76.3 %reduce-scatter.11.cloned.1.call-done = f32[256,1024]{1,0:T(8,128)} async-done(((f32[1024,1024]{1,0:T(8,128)}), f32[256,1024]{1,0:T(8,128)}) %reduce-scatter.11.cloned.1.call-update) | async-done | bytes 1048592 | tf_op jit(solution)/shard_map/reduce_scatter | solution.py:175
  699.0 43.7 %all-reduce = (f32[1024]{0:T(1024)}, f32[1024]{0:T(1024)}) all-reduce(f32[1024]{0:T(1024)S(1)} %get-tuple-element.26, f32[1024]{0:T(1024)S(1)} %get-tuple-element.24), channel_id=1, replica_groups=mesh['dp'=8,'mp'=4] {'dp','mp'}, use_global_device_ids=true, to_apply=%region_21.22 | all-reduce | flops 2048 | bytes 16384 | tf_op jit(solution)/shard_map/psum | solution.py:183
  (166 shorter events, 96.8 us)
Async XLA Ops:
  7.2 239.3 %copy-start = (bf16[1024,1024]{1,0:T(8,128)(2,1)S(1)}, bf16[1024,1024]{1,0:T(8,128)(2,1)}, u32[]{:S(2)}) copy-start(bf16[1024,1024]{1,0:T(8,128)(2,1)} %param.13) | copy-start | bytes 6291460
  7.2 52.3 %all-gather.4.cloned.1.call-start = ((), (), s32[]{:S(2)}) async-start(), calls=%async_computation.4 | async-start | bytes 2621440 | tf_op jit(solution)/shard_map/all_gather | solution.py:50
  10.7 148.0 %reduce-scatter.5.cloned.1.call-start = ((), (), s32[]{:S(2)}) async-start(), calls=%async_computation.5 | async-start | bytes 5242880 | tf_op jit(solution)/shard_map/reduce_scatter | solution.py:84
  14.7 61.8 %copy-start.9 = (pred[512,1024]{1,0:T(8,128)(4,1)}, pred[512,1024]{1,0:T(8,128)(4,1)S(1)}, u32[]{:S(2)}) copy-start(pred[512,1024]{1,0:T(8,128)(4,1)S(1)} %get-tuple-element.44) | copy-start | bytes 1572868
  63.5 12.9 %copy-start.30 = (bf16[1,1024,256]{1,2,0:T(8,128)(2,1)}, bf16[1,1024,256]{1,2,0:T(8,128)(2,1)S(1)}, u32[]{:S(2)}) copy-start(bf16[1,1024,256]{1,2,0:T(8,128)(2,1)S(1)} %get-tuple-element.39) | copy-start | bytes 1572868
  83.0 77.2 %copy-start.32 = (f32[1024]{0:T(1024)S(1)}, f32[1024]{0:T(1024)}, u32[]{:S(2)}) copy-start(f32[1024]{0:T(1024)} %param.16) | copy-start | bytes 12292
  83.0 163.5 %all-gather.6.cloned.1.call-start = ((), (), s32[]{:S(2)}) async-start(), calls=%async_computation.6 | async-start | bytes 2621440 | tf_op jit(solution)/shard_map/all_gather | solution.py:87
  161.2 178.4 %reduce-scatter.9.cloned.1.call-start = ((), (), s32[]{:S(2)}) async-start(), calls=%async_computation.8 | async-start | bytes 5242880 | tf_op jit(solution)/shard_map/reduce_scatter | solution.py:114
  161.2 19.7 %collective-permute-start = (bf16[256,1024]{1,0:T(8,128)(2,1)}, bf16[256,1024]{1,0:T(8,128)(2,1)S(1)}, u32[]{:S(2)}, u32[]{:S(2)}) collective-permute-start(bf16[256,1024]{1,0:T(8,128)(2,1)} %param.17), channel_id=1, source_target_pairs={{0,1},{1,2},{2,3},{3,0},{4,5},{5,6},{6,7},{7,4},{8,9},{9,10},{10,1... | collective-permute-start | bytes 1572872 | tf_op jit(solution)/shard_map/ppermute | solution.py:103
  181.8 27.4 %collective-permute-start.1 = (bf16[256,1024]{1,0:T(8,128)(2,1)S(1)}, bf16[256,1024]{1,0:T(8,128)(2,1)}, u32[]{:S(2)}, u32[]{:S(2)}) collective-permute-start(bf16[256,1024]{1,0:T(8,128)(2,1)S(1)} %collective-permute-done), channel_id=1, source_target_pairs={{0,1},{1,2},{2,3},{3,0},{4,5},{5,6},{6,7},{7,4},{8,9},{9,10},{10,1... | collective-permute-start | bytes 1572872 | tf_op jit(solution)/shard_map/ppermute | solution.py:103
  209.2 24.4 %collective-permute-start.2 = (bf16[256,1024]{1,0:T(8,128)(2,1)}, bf16[256,1024]{1,0:T(8,128)(2,1)}, u32[]{:S(2)}, u32[]{:S(2)}) collective-permute-start(bf16[256,1024]{1,0:T(8,128)(2,1)} %collective-permute-done.1), channel_id=1, source_target_pairs={{0,1},{1,2},{2,3},{3,0},{4,5},{5,6},{6,7},{7,4},{8,9},{9,10},{10,1... | collective-permute-start | bytes 1572872 | tf_op jit(solution)/shard_map/ppermute | solution.py:103
  222.0 22.8 %copy-start.23 = (bf16[256,1024]{1,0:T(8,128)(2,1)S(1)}, bf16[256,1024]{1,0:T(8,128)(2,1)}, u32[]{:S(2)}) copy-start(bf16[256,1024]{1,0:T(8,128)(2,1)} %copy-done.22) | copy-start | bytes 1572868
  222.0 23.6 %copy-start.13 = (bf16[256,1024]{1,0:T(8,128)(2,1)S(1)}, bf16[256,1024]{1,0:T(8,128)(2,1)}, u32[]{:S(2)}) copy-start(bf16[256,1024]{1,0:T(8,128)(2,1)} %param.17) | copy-start | bytes 1572868
  264.2 76.9 %copy-start.14 = (bf16[256,1024]{1,0:T(8,128)(2,1)S(1)}, bf16[256,1024]{1,0:T(8,128)(2,1)}, u32[]{:S(2)}) copy-start(bf16[256,1024]{1,0:T(8,128)(2,1)} %param.17) | copy-start | bytes 1572868
  264.3 125.8 %all-gather.8.cloned.1.call-start = ((), (), s32[]{:S(2)}) async-start(), calls=%async_computation.9 | async-start | bytes 2621440 | tf_op jit(solution)/shard_map/all_gather | solution.py:122
  343.5 274.1 %all-reduce.4.cloned.1.call-start = ((), (), s32[]{:S(2)}) async-start(), calls=%async_computation.11 | async-start | bytes 25165824 | tf_op jit(solution)/shard_map/psum | solution.py:184
  350.5 39.6 %copy-start.26 = (bf16[256,1024]{1,0:T(8,128)(2,1)S(1)}, bf16[256,1024]{1,0:T(8,128)(2,1)}, u32[]{:S(2)}) copy-start(bf16[256,1024]{1,0:T(8,128)(2,1)} %param.12) | copy-start | bytes 1572868
  357.1 35.5 %copy-start.12 = (pred[512,1024]{1,0:T(8,128)(4,1)S(1)}, pred[512,1024]{1,0:T(8,128)(4,1)}, u32[]{:S(2)}) copy-start(pred[512,1024]{1,0:T(8,128)(4,1)} %get-tuple-element.45) | copy-start | bytes 1572868
  445.3 252.1 %reduce-scatter.11.cloned.1.call-start = ((), (), s32[]{:S(2)}) async-start(), calls=%async_computation.10 | async-start | bytes 5242880 | tf_op jit(solution)/shard_map/reduce_scatter | solution.py:175
  451.6 293.6 %reduce-scatter.7.cloned.1.call-start = ((), (), s32[]{:S(2)}) async-start(), calls=%async_computation.7 | async-start | bytes 2621440 | tf_op jit(solution)/shard_map/reduce_scatter | solution.py:90
  459.4 238.1 %copy-start.7 = (bf16[256,1024]{1,0:T(8,128)(2,1)S(1)}, bf16[256,1024]{1,0:T(8,128)(2,1)}, u32[]{:S(2)}) copy-start(bf16[256,1024]{1,0:T(8,128)(2,1)} %param.9) | copy-start | bytes 1572868
  459.4 238.1 %copy-start.33 = (f32[1024]{0:T(1024)S(1)}, f32[1024]{0:T(1024)}, u32[]{:S(2)}) copy-start(f32[1024]{0:T(1024)} %param.15) | copy-start | bytes 12292
  459.4 285.7 %copy-start.8 = (f32[256,1024]{1,0:T(8,128)S(1)}, f32[256,1024]{1,0:T(8,128)}, u32[]{:S(2)}) copy-start(f32[256,1024]{1,0:T(8,128)} %reduce-scatter.9.cloned.1.call-done) | copy-start | bytes 3145732
  459.4 285.7 %copy-start.15 = (bf16[256,1024]{1,0:T(8,128)(2,1)S(1)}, bf16[256,1024]{1,0:T(8,128)(2,1)}, u32[]{:S(2)}) copy-start(bf16[256,1024]{1,0:T(8,128)(2,1)} %param.17) | copy-start | bytes 1572868
  (30 other events, 147.5 us)
Sparse Core Ops, SparseCore 0:
  10.8 48.6 all-gather.3
  83.1 75.4 reduce-scatter.4
  161.3 62.1 all-gather.5
  264.4 75.1 reduce-scatter.8
  343.6 46.4 all-gather.7
  445.4 172.0 all-reduce.3
  620.6 76.8 reduce-scatter.10
  699.8 45.3 reduce-scatter.6
